TPU v7x, 128 devices: a whole 4x4x4 slice. The times are simulated.
128 devices in a mesh: seg: 4 (over y), expert: 32 (over x, z, core).
Axes of the slice: x: 4, y: 4, z: 4, core: 2. Of those that a mesh axis runs over, the one named last changes fastest.
Arguments:
- frames: bfloat16 [32768, 1536], P(('seg', 'expert')), may hold values from -6 to 6
- expert_ids: int32 [32768, 2], P(('seg', 'expert')), may hold values from 0 to 31, all different within a row; in each aligned block of 256 rows (0 to 255, 256 to 511, ...) at most 24 rows name the same one
- gate_weights: float32 [32768, 2], P(('seg', 'expert')), may hold values from 0.2 to 1
- up_weight: bfloat16 [32, 1536, 2048], P('expert'), may hold values from -0.15625 to 0.15625
- down_weight: bfloat16 [32, 2048, 1536], P('expert'), may hold values from -0.125 to 0.125
- out_weight: bfloat16 [1536, 64], replicated, may hold values from -0.15625 to 0.15625
- in_conv: bfloat16 [7, 64, 2048], replicated, may hold values from -0.25 to 0.25
- snake_first: float32 [2048], replicated, may hold values from 0.5 to 2
- first_up: bfloat16 [16, 2048, 512], P(None, None, 'seg'), may hold values from -0.09375 to 0.09375
Outputs:
- features: float32 [4, 65536, 512], P(None, 'expert', 'seg')
Inputs may be any that keep to these rules, and one draw needn't show every extreme that they name: `expert_ids`: in each aligned block of 256 rows (the rows of one device) no expert is named by more than 24 of the block's choices, and some block reaches 24; the two ids of a token differ.
All inputs are finite; a program needn't handle non-finite values.
Results may differ from a plain program's by a relative error of at most 0.005.
Values may be sent and summed in bfloat16 or wider, within the bound.
A program may use at most 128 MiB of HBM per device.

v0:
```python
import jax
import jax.numpy as jnp
from jax import lax
from jax.sharding import PartitionSpec as P


def with_halo(value, sides, width):
    for axis, dim in sides:
        size, length = (lax.axis_size(axis), value.shape[dim])
        up = [(i, (i + 1) % size) for i in range(size - 1)]
        down = [(j, i) for i, j in up]
        last = lax.slice_in_dim(value, length - width, length, axis=dim)
        leading = lax.slice_in_dim(value, 0, width, axis=dim)
        before = lax.ppermute(last, axis, up)
        after = lax.ppermute(leading, axis, down)
        value = jnp.concatenate([before, value, after], axis=dim)
    return value


def snake_act(values, alpha_row):
    return values + jnp.sin(alpha_row * values) ** 2 / alpha_row


def slot_dest(expert_ids, num_experts, capacity):
    flat_ids = expert_ids.reshape(-1)
    one_hot = (flat_ids[:, None] == jnp.arange(num_experts, dtype=jnp.int32)[None, :]).astype(
        jnp.int32
    )
    before = jnp.cumsum(one_hot, axis=0) - one_hot
    return flat_ids * capacity + jnp.sum(before * one_hot, axis=1)


def conv_seven(padded, weights, length):
    windows = [
        lax.slice_in_dim(padded, tap_index, tap_index + length, axis=1) for tap_index in range(7)
    ]
    stacked = jnp.concatenate(windows, axis=2)
    return jnp.einsum(
        "klc,co->klo",
        stacked,
        weights.reshape(-1, weights.shape[2]),
        preferred_element_type=jnp.float32,
    )


def upsample(padded, weights, length):
    prev_rows = padded[:, 0:length]
    here_rows = padded[:, 1 : length + 1]
    next_rows = padded[:, 2 : length + 2]
    middle = jnp.einsum(
        "klc,rco->klro", here_rows, weights[4:12], preferred_element_type=jnp.float32
    )
    early_part = jnp.einsum(
        "klc,rco->klro", prev_rows, weights[12:16], preferred_element_type=jnp.float32
    )
    later_part = jnp.einsum(
        "klc,rco->klro", next_rows, weights[0:4], preferred_element_type=jnp.float32
    )
    joined = middle + jnp.concatenate([early_part, later_part], axis=2)
    return joined.reshape(padded.shape[0], length * 8, weights.shape[2])


def local(
    frames,
    expert_ids,
    gate_weights,
    up_weight,
    down_weight,
    out_weight,
    in_conv,
    snake_first,
    first_up,
):
    tok_rows, model_dim = frames.shape
    num_experts = lax.axis_size("expert")
    capacity = 3 * tok_rows // num_experts
    dest_slot = slot_dest(expert_ids, num_experts, capacity)
    source_rows = jnp.repeat(frames, 2, axis=0)
    send_buffer = (
        jnp.zeros((num_experts * capacity, model_dim), jnp.bfloat16).at[dest_slot].set(source_rows)
    )
    send_buffer = send_buffer.reshape(num_experts, capacity, model_dim)
    upper_weight = up_weight[0]
    lower_weight = down_weight[0]
    received = lax.all_to_all(send_buffer, "expert", split_axis=0, concat_axis=0, tiled=True)
    count_src, count_rows, _ = received.shape
    flat_rows = received.reshape(count_src * count_rows, model_dim)
    hidden_units = jax.nn.gelu(
        jnp.dot(flat_rows, upper_weight, preferred_element_type=jnp.float32), approximate=True
    ).astype(jnp.bfloat16)
    expert_out = jnp.dot(hidden_units, lower_weight, preferred_element_type=jnp.float32).astype(
        jnp.bfloat16
    )
    processed = expert_out.reshape(count_src, count_rows, expert_out.shape[1])
    returned = lax.all_to_all(processed, "expert", split_axis=0, concat_axis=0, tiled=True)
    picked_rows = returned.reshape(num_experts * capacity, model_dim)[dest_slot]
    picked = jnp.dot(picked_rows, out_weight, preferred_element_type=jnp.float32)
    lat_dim = out_weight.shape[1]
    gated = jnp.sum(picked.reshape(tok_rows, 2, lat_dim) * gate_weights[:, :, None], axis=1)
    latent = jnp.dot(frames, out_weight, preferred_element_type=jnp.float32) + gated
    latent_low = latent.astype(jnp.bfloat16)
    lat_padded = with_halo(latent_low, (("expert", 0),), 3)
    first_in = conv_seven(lat_padded[None], in_conv, tok_rows)[0]
    act_first = snake_act(first_in, snake_first).astype(jnp.bfloat16)
    pad_first = with_halo(act_first, (("expert", 0),), 1)
    return upsample(lax.all_gather(pad_first[None], "seg", axis=0, tiled=True), first_up, tok_rows)


def solution(mesh):
    placed = (
        P(("seg", "expert"), None),
        P(("seg", "expert"), None),
        P(("seg", "expert"), None),
        P("expert", None, None),
        P("expert", None, None),
        P(),
        P(),
        P(),
        P(None, None, "seg"),
    )
    return jax.shard_map(
        local, mesh=mesh, in_specs=placed, out_specs=P(None, "expert", "seg"), check_vma=False
    )
```

profile of v0, /device:TPU:1, one launch (start us, length us, event | category | flops | bytes accessed | tf_op | source)
XLA Modules:
  0.0 225.3 jit_solution(10748287871956991975)
XLA Ops:
  6.5 0.8 broadcast_multiply_fusion
  7.4 0.8 copy.19
  8.2 0.1 eq.29
  8.3 0.1 eq.25
  8.5 0.1 copy.18
  8.6 0.1 mul.58
  8.8 1.2 reduce-window.6
  9.9 0.2 slice_reduce_fusion
  10.2 2.0 broadcast_in_dim.9
  12.2 1.5 reshape.99
  13.7 0.1 fusion.44
  13.8 5.5 %scatter_custom_fusion = bf16[768,1536]{1,0:T(8,128)(2,1)} fusion(s32[512]{0:T(512)S(1)} %bitcast.91, bf16[512,1536]{1,0:T(8,128)(2,1)} %reshape.99, bf16[]{:T(256)} %constant.9.clone.1), kind=kCustom, calls=%fused_computation.35 | custom fusion | bytes 2359808 | tf_op jit(solution)/shard_map/scatter | solution.py:80
  19.3 41.0 %all_to_all.10 = bf16[32,24,1536]{2,1,0:T(8,128)(2,1)} all-to-all(bf16[32,24,1536]{2,1,0:T(8,128)(2,1)} %bitcast.87), channel_id=1, replica_groups=mesh['seg'=4,'expert'=32] {'expert'}, dimensions={0} | all-to-all | bytes 4718592 | tf_op jit(solution)/shard_map/all_to_all | solution.py:85
  60.3 16.6 %fusion.17 = bf16[768,1536]{1,0:T(8,128)(2,1)} fusion(bf16[1,2048,1536]{2,1,0:T(8,128)(2,1)} %param.13, bf16[768,1536]{1,0:T(8,128)(2,1)} %bitcast.89, bf16[1,1536,2048]{2,1,0:T(8,128)(2,1)} %param.12), kind=kOutput, calls=%fused_computation.25 | convolution fusion | flops 9679011840 | bytes 17301504 | tf_op jit(solution)/shard_map/dot_general | solution.py:91
  76.9 4.7 %all-to-all-start.1 = ((bf16[32,24,1536]{2,1,0:T(8,128)(2,1)}), bf16[32,24,1536]{2,1,0:T(8,128)(2,1)}, u32[]{:S(2)}, u32[]{:S(2)}) async-start(bf16[32,24,1536]{2,1,0:T(8,128)(2,1)} %bitcast.88), calls=%async_computation.1 | async-start | bytes 4718592 | tf_op jit(solution)/shard_map/all_to_all | solution.py:95
  81.6 0.0 all-gather.4.cloned.1.call-start
  81.7 0.1 copy.23
  81.9 31.1 %all-to-all-done.1 = bf16[32,24,1536]{2,1,0:T(8,128)(2,1)} async-done(((bf16[32,24,1536]{2,1,0:T(8,128)(2,1)}), bf16[32,24,1536]{2,1,0:T(8,128)(2,1)}, u32[]{:S(2)}, u32[]{:S(2)}) %all-to-all-start.1) | async-done | bytes 2359328 | tf_op jit(solution)/shard_map/all_to_all | solution.py:95
  112.9 5.6 %gather_fusion = bf16[512,1536]{1,0:T(8,128)(2,1)S(1)} fusion(bf16[768,1536]{1,0:T(8,128)(2,1)} %bitcast.8, s32[1024]{0:T(1024)S(1)} %pad_clamp_fusion), kind=kCustom, calls=%fused_computation | custom fusion | bytes 3147776 | tf_op jit(solution)/shard_map/gather | solution.py:96
  118.5 0.0 copy-start.3
  118.5 1.5 fusion.52
  120.0 0.4 multiply_reduce_fusion
  120.4 0.1 copy.24
  120.5 1.5 fusion.37
  122.0 0.1 fusion.51
  122.1 2.4 %collective-permute-start = (bf16[3,64]{0,1:T(8,128)(2,1)S(1)}, bf16[3,64]{0,1:T(8,128)(2,1)S(1)}, u32[]{:S(2)}, u32[]{:S(2)}) collective-permute-start(bf16[3,64]{0,1:T(8,128)(2,1)S(1)} %get-tuple-element.7), channel_id=1, source_target_pairs={{0,1},{1,2},{2,3},{3,4},{4,5},{5,6},{6,7},{7,8},{8,9},{9,10},{10,1... | collective-permute-start | bytes 1160 | tf_op jit(solution)/shard_map/ppermute | solution.py:14
  124.5 2.2 collective-permute-start.1
  126.7 2.9 %collective-permute-done.1 = bf16[3,64]{0,1:T(8,128)(2,1)S(1)} collective-permute-done((bf16[3,64]{0,1:T(8,128)(2,1)S(1)}, bf16[3,64]{0,1:T(8,128)(2,1)S(1)}, u32[]{:S(2)}, u32[]{:S(2)}) %collective-permute-start.1) | collective-permute-done | bytes 416 | tf_op jit(solution)/shard_map/ppermute | solution.py:15
  129.5 0.1 maximum_bitcast_fusion.1
  129.7 0.1 slice_dynamic-update-slice_fusion.5
  129.7 0.1 slice_dynamic-update-slice_fusion.4
  129.8 0.1 slice_dynamic-update-slice_fusion.3
  129.9 0.1 slice_dynamic-update-slice_fusion.2
  130.0 0.1 slice_dynamic-update-slice_fusion.1
  130.1 0.1 slice_dynamic-update-slice_fusion
  130.1 0.0 copy-done.3
  130.2 8.7 %add_convert_fusion = bf16[256,2048]{1,0:T(8,128)(2,1)S(1)} fusion(f32[2048]{0:T(1024)S(1)} %copy-done.3, bf16[448,2048]{1,0:T(8,128)(2,1)S(1)} %bitcast.86, bf16[1,256,448]{1,2,0:T(8,128)(2,1)S(1)} %slice_dynamic-update-slice_fusion), kind=kOutput, calls=%fused_computation.34 | convolution fusion | flops 472383488 | bytes 3121152 | tf_op jit(solution)/shard_map/klc,co->klo/dot_general | solution.py:38
  138.9 1.9 collective-permute-start.2
  140.9 2.4 %collective-permute-start.3 = (bf16[1,2048]{1,0:T(2,128)(2,1)S(1)}, bf16[1,2048]{1,0:T(2,128)(2,1)S(1)}, u32[]{:S(2)}, u32[]{:S(2)}) collective-permute-start(bf16[1,2048]{1,0:T(2,128)(2,1)S(1)} %get-tuple-element.6), channel_id=1, source_target_pairs={{1,0},{2,1},{3,2},{4,3},{5,4},{6,5},{7,6},{8,7},{9,8},{10,9},{11,1... | collective-permute-start | bytes 12296 | tf_op jit(solution)/shard_map/ppermute | solution.py:15
  143.3 2.6 %collective-permute-done.3 = bf16[1,2048]{1,0:T(2,128)(2,1)S(1)} collective-permute-done((bf16[1,2048]{1,0:T(2,128)(2,1)S(1)}, bf16[1,2048]{1,0:T(2,128)(2,1)S(1)}, u32[]{:S(2)}, u32[]{:S(2)}) %collective-permute-start.3) | collective-permute-done | bytes 4128 | tf_op jit(solution)/shard_map/ppermute | solution.py:15
  145.8 1.3 maximum_bitcast_fusion
  147.1 0.0 all-gather.4.cloned.1.call-update
  147.2 52.8 %all-gather.4.cloned.1.call-done = bf16[4,258,2048]{2,1,0:T(8,128)(2,1)} async-done(((bf16[1,258,2048]{2,1,0:T(8,128)(2,1)}), bf16[4,258,2048]{2,1,0:T(8,128)(2,1)}) %all-gather.4.cloned.1.call-update) | async-done | bytes 4227088 | tf_op jit(solution)/shard_map/all_gather | solution.py:106
  200.0 5.3 %fusion.13 = f32[4,256,4,128]{3,1,2,0:T(8,128)S(1)} fusion(bf16[4,258,2048]{2,1,0:T(8,128)(2,1)} %all-gather.4.cloned.1.call-done, bf16[16,2048,128]{2,1,0:T(8,128)(2,1)} %param.17), kind=kOutput, calls=%fused_computation.18 | convolution fusion | flops 2147483648 | bytes 8388608 | tf_op jit(solution)/shard_map/klc,rco->klro/dot_general | solution.py:53
  205.3 0.0 slice-start.1
  205.3 4.1 %fusion.12 = f32[4,256,4,128]{3,1,2,0:T(8,128)S(1)} fusion(bf16[4,258,2048]{2,1,0:T(8,128)(2,1)S(1)} %copy-done.2, bf16[16,2048,128]{2,1,0:T(8,128)(2,1)} %param.17), kind=kOutput, calls=%fused_computation.16 | convolution fusion | flops 2147483648 | bytes 8388608 | tf_op jit(solution)/shard_map/klc,rco->klro/dot_general | solution.py:56
  209.5 4.5 %maximum_add_fusion = f32[4,256,8,128]{3,1,2,0:T(8,128)S(1)} fusion(f32[4,256,4,128]{3,1,2,0:T(8,128)S(1)} %fusion.12, f32[4,256,4,128]{3,1,2,0:T(8,128)S(1)} %fusion.13, bf16[16,2048,128]{2,1,0:T(8,128)(2,1)S(1)} %bitcast.95, bf16[4,258,2048]{2,1,0:T(8,128)(2,1)S(1)} %copy-done.2), kind=kOutput, calls=%fused_computation.21 | convolution fusion | flops 4297064448 | bytes 16777216 | tf_op jit(solution)/shard_map/klc,rco->klro/dot_general | solution.py:50
  214.0 4.4 %copy.33 = f32[4,256,8,128]{3,2,1,0:T(8,128)} copy(f32[4,256,8,128]{3,1,2,0:T(8,128)S(1)} %maximum_add_fusion) | data formatting | bytes 8388608 | tf_op jit(solution)/shard_map/add | solution.py:59
  (19 shorter events, 0.1 us)
Async XLA Ops:
  6.5 123.6 %copy-start = (bf16[7,64,2048]{2,1,0:T(8,128)(2,1)S(1)}, bf16[7,64,2048]{2,1,0:T(8,128)(2,1)}, u32[]{:S(2)}) copy-start(bf16[7,64,2048]{2,1,0:T(8,128)(2,1)} %param.15) | copy-start | bytes 5505028
  76.9 4.8 %copy-start.1 = (f32[256,2]{0,1:T(2,128)S(1)}, f32[256,2]{0,1:T(2,128)}, u32[]{:S(2)}) copy-start(f32[256,2]{0,1:T(2,128)} %param.11) | copy-start | bytes 6148
  76.9 36.0 %all-to-all-start.1 = ((bf16[32,24,1536]{2,1,0:T(8,128)(2,1)}), bf16[32,24,1536]{2,1,0:T(8,128)(2,1)}, u32[]{:S(2)}, u32[]{:S(2)}) async-start(bf16[32,24,1536]{2,1,0:T(8,128)(2,1)} %bitcast.88), calls=%async_computation.1 | async-start | bytes 4718592 | tf_op jit(solution)/shard_map/all_to_all | solution.py:95
  81.6 118.3 %all-gather.4.cloned.1.call-start = ((), (), s32[]{:S(2)}) async-start(), calls=%async_computation.2 | async-start | bytes 5406720 | tf_op jit(solution)/shard_map/all_gather | solution.py:106
  118.5 11.6 %copy-start.3 = (f32[2048]{0:T(1024)S(1)}, f32[2048]{0:T(1024)}, u32[]{:S(2)}) copy-start(f32[2048]{0:T(1024)} %param.16) | copy-start | bytes 24580
  122.1 4.6 %collective-permute-start = (bf16[3,64]{0,1:T(8,128)(2,1)S(1)}, bf16[3,64]{0,1:T(8,128)(2,1)S(1)}, u32[]{:S(2)}, u32[]{:S(2)}) collective-permute-start(bf16[3,64]{0,1:T(8,128)(2,1)S(1)} %get-tuple-element.7), channel_id=1, source_target_pairs={{0,1},{1,2},{2,3},{3,4},{4,5},{5,6},{6,7},{7,8},{8,9},{9,10},{10,1... | collective-permute-start | bytes 1160 | tf_op jit(solution)/shard_map/ppermute | solution.py:14
  124.5 5.1 %collective-permute-start.1 = (bf16[3,64]{0,1:T(8,128)(2,1)S(1)}, bf16[3,64]{0,1:T(8,128)(2,1)S(1)}, u32[]{:S(2)}, u32[]{:S(2)}) collective-permute-start(bf16[3,64]{0,1:T(8,128)(2,1)S(1)} %get-tuple-element.8), channel_id=1, source_target_pairs={{1,0},{2,1},{3,2},{4,3},{5,4},{6,5},{7,6},{8,7},{9,8},{10,9},{11,1... | collective-permute-start | bytes 1160 | tf_op jit(solution)/shard_map/ppermute | solution.py:15
  138.9 4.3 %collective-permute-start.2 = (bf16[1,2048]{1,0:T(2,128)(2,1)S(1)}, bf16[1,2048]{1,0:T(2,128)(2,1)S(1)}, u32[]{:S(2)}, u32[]{:S(2)}) collective-permute-start(bf16[1,2048]{1,0:T(2,128)(2,1)S(1)} %get-tuple-element.5), channel_id=1, source_target_pairs={{0,1},{1,2},{2,3},{3,4},{4,5},{5,6},{6,7},{7,8},{8,9},{9,10},{10,1... | collective-permute-start | bytes 12296 | tf_op jit(solution)/shard_map/ppermute | solution.py:14
  140.9 5.0 %collective-permute-start.3 = (bf16[1,2048]{1,0:T(2,128)(2,1)S(1)}, bf16[1,2048]{1,0:T(2,128)(2,1)S(1)}, u32[]{:S(2)}, u32[]{:S(2)}) collective-permute-start(bf16[1,2048]{1,0:T(2,128)(2,1)S(1)} %get-tuple-element.6), channel_id=1, source_target_pairs={{1,0},{2,1},{3,2},{4,3},{5,4},{6,5},{7,6},{8,7},{9,8},{10,9},{11,1... | collective-permute-start | bytes 12296 | tf_op jit(solution)/shard_map/ppermute | solution.py:15
  200.0 5.3 %copy-start.2 = (bf16[4,258,2048]{2,1,0:T(8,128)(2,1)S(1)}, bf16[4,258,2048]{2,1,0:T(8,128)(2,1)}, u32[]{:S(2)}) copy-start(bf16[4,258,2048]{2,1,0:T(8,128)(2,1)} %all-gather.4.cloned.1.call-done) | copy-start | bytes 12681220
  200.0 9.4 %slice-start = ((s8[8388608]{0:T(1024)(128)(4,1)}), s8[4194304]{0:T(1024)(128)(4,1)S(1)}, s32[]{:S(2)}) async-start(s8[8388608]{0:T(1024)(128)(4,1)} %bitcast.94), calls=%async_computation.3 | async-start | bytes 8388608
  205.3 4.1 %slice-start.1 = ((s8[8388608]{0:T(1024)(128)(4,1)}), s8[4194304]{0:T(1024)(128)(4,1)S(1)}, s32[]{:S(2)}) async-start(s8[8388608]{0:T(1024)(128)(4,1)} %bitcast.94), calls=%async_computation.4 | async-start | bytes 8388608
Sparse Core Ops, SparseCore 0:
  147.3 52.6 all-gather.3
where the time goes:
time: 226 us; the launch traced here: 225 us
  waiting for transfers between devices  89.4 us (40%)
  matrix products  42.3 us (19%)
  blocking collectives  41 us (18%)
  local copies, waits for them, and re-layouts  21.4 us (9%)
  between operations  13.7 us (6%)
  starting transfers between devices  13.6 us (6%)
  other arithmetic  3.95 us (2%)
    all_gather x1, waiting for transfers between devices, local(): lax.all_gather(pad_first[None], 'seg', axis=0, tiled=True)  52.8 us
    all_to_all x1, blocking collectives, local(): lax.all_to_all(send_buffer, 'expert', split_axis=0, concat_axis=0, tiled=...  41 us
    all_to_all x1, waiting for transfers between devices, local(): lax.all_to_all(processed, 'expert', split_axis=0, concat_axis=0, tiled=True)  31.1 us
    dot_general x1, matrix products, local(): jnp.dot(hidden_units, lower_weight, preferred_element_type=jnp.float32)  16.6 us
    dot_general x1, matrix products, conv_seven(): jnp.einsum('klc,co->klo', stacked, weights.reshape(-1, weights.shape[2]),...  8.72 us
    gather x1, local copies, waits for them, and re-layouts, local(): picked_rows = returned.reshape(num_experts * capacity, model_dim)[dest_slot]  5.57 us
    scatter x1, local copies, waits for them, and re-layouts, local(): jnp.zeros((num_experts * capacity, model_dim), jnp.bfloat16).at[dest_slot]  5.52 us
    ppermute x2, waiting for transfers between devices, with_halo(): after = lax.ppermute(leading, axis, down)  5.43 us
  transfers between devices with their start and end apart: 6, of which 4 were waited for; matrix products, arithmetic and copies ran while one was open for 0% of the time, Pallas kernels for 0%

commit v1 on v0

--- a/solution.py
+++ b/solution.py
@@ -103,7 +103,13 @@
     first_in = conv_seven(lat_padded[None], in_conv, tok_rows)[0]
     act_first = snake_act(first_in, snake_first).astype(jnp.bfloat16)
     pad_first = with_halo(act_first, (("expert", 0),), 1)
-    return upsample(lax.all_gather(pad_first[None], "seg", axis=0, tiled=True), first_up, tok_rows)
+    return upsample(
+        jnp.concatenate(
+            lax.all_to_all(jnp.stack([pad_first[None]] * lax.axis_size("seg")), "seg", 0, 0), axis=0
+        ),
+        first_up,
+        tok_rows,
+    )
 
 
 def solution(mesh):

time: 226 us -> 208 us (0.920)
  blocking collectives: 41 us -> 95 us
  waiting for transfers between devices: 89.4 us -> 36.5 us
  between operations: 13.7 us -> 0.25 us
  matrix products: 42.3 us -> 37.6 us
    all_to_all x0 -> x1, blocking collectives: none -> 54 us  [local(): lax.all_to_all(jnp.stack([pad_first[None]] * lax.axis_size('seg')), 'seg'...]
    all_gather x1 -> x0, waiting for transfers between devices: 52.8 us -> none  [local(): lax.all_gather(pad_first[None], 'seg', axis=0, tiled=True)]
    dot_general x1, matrix products: 5.32 us -> 2.32 us  [upsample(): jnp.einsum('klc,rco->klro', prev_rows, weights[12:16], preferred_element_...]
  transfers between devices with their start and end apart: 6 -> 5, of which waited for: 4 -> 3; matrix products, arithmetic and copies ran while one was open for 0% -> 0% of each run, Pallas kernels for 0% -> 0%
where the time goes in v1:
time: 208 us
  blocking collectives  95 us (46%)
  matrix products  37.6 us (18%)
  waiting for transfers between devices  36.5 us (18%)
  local copies, waits for them, and re-layouts  22 us (11%)
  starting transfers between devices  13.6 us (7%)
  other arithmetic  2.92 us (1%)
    all_to_all x1, blocking collectives, local(): lax.all_to_all(jnp.stack([pad_first[None]] * lax.axis_size('seg')), 'seg'...  54 us
    all_to_all x1, blocking collectives, local(): lax.all_to_all(send_buffer, 'expert', split_axis=0, concat_axis=0, tiled=...  41 us
    all_to_all x1, waiting for transfers between devices, local(): lax.all_to_all(processed, 'expert', split_axis=0, concat_axis=0, tiled=True)  31.1 us
    dot_general x1, matrix products, local(): jnp.dot(hidden_units, lower_weight, preferred_element_type=jnp.float32)  16.6 us
    dot_general x1, matrix products, conv_seven(): jnp.einsum('klc,co->klo', stacked, weights.reshape(-1, weights.shape[2]),...  8.72 us
    gather x1, local copies, waits for them, and re-layouts, local(): picked_rows = returned.reshape(num_experts * capacity, model_dim)[dest_slot]  5.57 us
    scatter x1, local copies, waits for them, and re-layouts, local(): jnp.zeros((num_experts * capacity, model_dim), jnp.bfloat16).at[dest_slot]  5.52 us
    ppermute x2, waiting for transfers between devices, with_halo(): after = lax.ppermute(leading, axis, down)  5.41 us
  transfers between devices with their start and end apart: 5, of which 3 were waited for; matrix products, arithmetic and copies ran while one was open for 0% of the time, Pallas kernels for 0%

profile of v1, /device:TPU:1, one launch (start us, length us, event | category | flops | bytes accessed | tf_op | source)
XLA Modules:
  0.0 207.8 jit_solution(7015443123860901873)
XLA Ops:
  0.0 0.8 broadcast_multiply_fusion
  0.8 0.8 copy.19
  1.6 0.1 eq.29
  1.8 0.1 eq.25
  1.9 0.1 copy.18
  2.1 0.1 mul.58
  2.2 1.2 reduce-window.6
  3.4 0.2 slice_reduce_fusion
  3.7 2.0 broadcast_in_dim.7
  5.6 1.5 reshape.105
  7.2 0.1 fusion.44
  7.3 5.5 %scatter_custom_fusion = bf16[768,1536]{1,0:T(8,128)(2,1)} fusion(s32[512]{0:T(512)S(1)} %bitcast.93, bf16[512,1536]{1,0:T(8,128)(2,1)} %reshape.105, bf16[]{:T(256)} %constant.9.clone.1), kind=kCustom, calls=%fused_computation.35 | custom fusion | bytes 2359808 | tf_op jit(solution)/shard_map/scatter | solution.py:80
  12.8 41.0 %all_to_all.15 = bf16[32,24,1536]{2,1,0:T(8,128)(2,1)} all-to-all(bf16[32,24,1536]{2,1,0:T(8,128)(2,1)} %bitcast.86), channel_id=1, replica_groups=mesh['seg'=4,'expert'=32] {'expert'}, dimensions={0} | all-to-all | bytes 4718592 | tf_op jit(solution)/shard_map/all_to_all | solution.py:85
  53.7 16.6 %fusion.17 = bf16[768,1536]{1,0:T(8,128)(2,1)} fusion(bf16[1,2048,1536]{2,1,0:T(8,128)(2,1)} %param.13, bf16[768,1536]{1,0:T(8,128)(2,1)} %bitcast.91, bf16[1,1536,2048]{2,1,0:T(8,128)(2,1)} %param.12), kind=kOutput, calls=%fused_computation.25 | convolution fusion | flops 9679011840 | bytes 17301504 | tf_op jit(solution)/shard_map/dot_general | solution.py:91
  70.4 4.7 %all-to-all-start.1 = ((bf16[32,24,1536]{2,1,0:T(8,128)(2,1)}), bf16[32,24,1536]{2,1,0:T(8,128)(2,1)}, u32[]{:S(2)}, u32[]{:S(2)}) async-start(bf16[32,24,1536]{2,1,0:T(8,128)(2,1)} %bitcast.90), calls=%async_computation.1 | async-start | bytes 4718592 | tf_op jit(solution)/shard_map/all_to_all | solution.py:95
  75.1 0.1 copy.23
  75.3 31.1 %all-to-all-done.1 = bf16[32,24,1536]{2,1,0:T(8,128)(2,1)} async-done(((bf16[32,24,1536]{2,1,0:T(8,128)(2,1)}), bf16[32,24,1536]{2,1,0:T(8,128)(2,1)}, u32[]{:S(2)}, u32[]{:S(2)}) %all-to-all-start.1) | async-done | bytes 2359328 | tf_op jit(solution)/shard_map/all_to_all | solution.py:95
  106.4 5.6 %gather_fusion = bf16[512,1536]{1,0:T(8,128)(2,1)S(1)} fusion(bf16[768,1536]{1,0:T(8,128)(2,1)} %bitcast.8, s32[1024]{0:T(1024)S(1)} %pad_clamp_fusion), kind=kCustom, calls=%fused_computation | custom fusion | bytes 3147776 | tf_op jit(solution)/shard_map/gather | solution.py:96
  112.0 0.0 copy-start.2
  112.0 1.5 fusion.52
  113.5 0.4 multiply_reduce_fusion
  113.9 0.1 copy.24
  114.0 1.5 fusion.37
  115.5 0.1 fusion.51
  115.6 2.3 %collective-permute-start = (bf16[3,64]{0,1:T(8,128)(2,1)S(1)}, bf16[3,64]{0,1:T(8,128)(2,1)S(1)}, u32[]{:S(2)}, u32[]{:S(2)}) collective-permute-start(bf16[3,64]{0,1:T(8,128)(2,1)S(1)} %get-tuple-element.7), channel_id=1, source_target_pairs={{0,1},{1,2},{2,3},{3,4},{4,5},{5,6},{6,7},{7,8},{8,9},{9,10},{10,1... | collective-permute-start | bytes 1160 | tf_op jit(solution)/shard_map/ppermute | solution.py:14
  118.0 2.2 %collective-permute-start.1 = (bf16[3,64]{0,1:T(8,128)(2,1)S(1)}, bf16[3,64]{0,1:T(8,128)(2,1)S(1)}, u32[]{:S(2)}, u32[]{:S(2)}) collective-permute-start(bf16[3,64]{0,1:T(8,128)(2,1)S(1)} %get-tuple-element.8), channel_id=1, source_target_pairs={{1,0},{2,1},{3,2},{4,3},{5,4},{6,5},{7,6},{8,7},{9,8},{10,9},{11,1... | collective-permute-start | bytes 1160 | tf_op jit(solution)/shard_map/ppermute | solution.py:15
  120.2 0.0 collective-permute-done
  120.2 2.8 %collective-permute-done.1 = bf16[3,64]{0,1:T(8,128)(2,1)S(1)} collective-permute-done((bf16[3,64]{0,1:T(8,128)(2,1)S(1)}, bf16[3,64]{0,1:T(8,128)(2,1)S(1)}, u32[]{:S(2)}, u32[]{:S(2)}) %collective-permute-start.1) | collective-permute-done | bytes 416 | tf_op jit(solution)/shard_map/ppermute | solution.py:15
  123.0 0.1 maximum_bitcast_fusion
  123.1 0.1 slice_dynamic-update-slice_fusion.5
  123.2 0.1 slice_dynamic-update-slice_fusion.4
  123.3 0.1 slice_dynamic-update-slice_fusion.3
  123.4 0.1 slice_dynamic-update-slice_fusion.2
  123.4 0.1 slice_dynamic-update-slice_fusion.1
  123.5 0.1 slice_dynamic-update-slice_fusion
  123.6 0.0 copy-done.2
  123.6 8.7 %add_convert_fusion = bf16[256,2048]{1,0:T(8,128)(2,1)S(1)} fusion(f32[2048]{0:T(1024)S(1)} %copy-done.2, bf16[448,2048]{1,0:T(8,128)(2,1)S(1)} %bitcast.85, bf16[1,256,448]{1,2,0:T(8,128)(2,1)S(1)} %slice_dynamic-update-slice_fusion), kind=kOutput, calls=%fused_computation.34 | convolution fusion | flops 472383488 | bytes 3121152 | tf_op jit(solution)/shard_map/klc,co->klo/dot_general | solution.py:38
  132.4 1.9 collective-permute-start.2
  134.3 2.4 %collective-permute-start.3 = (bf16[1,2048]{1,0:T(2,128)(2,1)S(1)}, bf16[1,2048]{1,0:T(2,128)(2,1)S(1)}, u32[]{:S(2)}, u32[]{:S(2)}) collective-permute-start(bf16[1,2048]{1,0:T(2,128)(2,1)S(1)} %get-tuple-element.6), channel_id=1, source_target_pairs={{1,0},{2,1},{3,2},{4,3},{5,4},{6,5},{7,6},{8,7},{9,8},{10,9},{11,1... | collective-permute-start | bytes 12296 | tf_op jit(solution)/shard_map/ppermute | solution.py:15
  136.7 2.6 %collective-permute-done.3 = bf16[1,2048]{1,0:T(2,128)(2,1)S(1)} collective-permute-done((bf16[1,2048]{1,0:T(2,128)(2,1)S(1)}, bf16[1,2048]{1,0:T(2,128)(2,1)S(1)}, u32[]{:S(2)}, u32[]{:S(2)}) %collective-permute-start.3) | collective-permute-done | bytes 4128 | tf_op jit(solution)/shard_map/ppermute | solution.py:15
  139.3 0.3 pad_maximum_fusion
  139.6 0.5 stack.3
  140.1 0.0 slice-start.1
  140.1 54.0 %all_to_all.16 = bf16[4,1,258,2048]{3,2,1,0:T(8,128)(2,1)S(1)} all-to-all(bf16[4,1,258,2048]{3,2,1,0:T(8,128)(2,1)S(1)} %stack.3), channel_id=1, replica_groups=mesh['seg'=4,'expert'=32] {'seg'}, dimensions={0} | all-to-all | bytes 8454144 | tf_op jit(solution)/shard_map/all_to_all | solution.py:108
  194.2 2.3 %fusion.12 = f32[4,256,4,128]{3,1,2,0:T(8,128)S(1)} fusion(bf16[4,258,2048]{2,1,0:T(8,128)(2,1)S(1)} %bitcast.87, bf16[16,2048,128]{2,1,0:T(8,128)(2,1)S(1)} %bitcast.97), kind=kOutput, calls=%fused_computation.16 | convolution fusion | flops 2147483648 | bytes 8388608 | tf_op jit(solution)/shard_map/klc,rco->klro/dot_general | solution.py:56
  196.5 2.3 %fusion.13 = f32[4,256,4,128]{3,1,2,0:T(8,128)S(1)} fusion(bf16[4,258,2048]{2,1,0:T(8,128)(2,1)S(1)} %bitcast.88, bf16[16,2048,128]{2,1,0:T(8,128)(2,1)S(1)} %bitcast.97), kind=kOutput, calls=%fused_computation.18 | convolution fusion | flops 2147483648 | bytes 8388608 | tf_op jit(solution)/shard_map/klc,rco->klro/dot_general | solution.py:53
  198.9 4.5 %maximum_add_fusion = f32[4,256,8,128]{3,1,2,0:T(8,128)S(1)} fusion(f32[4,256,4,128]{3,1,2,0:T(8,128)S(1)} %fusion.12, f32[4,256,4,128]{3,1,2,0:T(8,128)S(1)} %fusion.13, bf16[16,2048,128]{2,1,0:T(8,128)(2,1)S(1)} %bitcast.97, bf16[4,258,2048]{2,1,0:T(8,128)(2,1)S(1)} %bitcast.89), kind=kOutput, calls=%fused_computation.21 | convolution fusion | flops 4297064448 | bytes 16777216 | tf_op jit(solution)/shard_map/klc,rco->klro/dot_general | solution.py:50
  203.4 4.4 %copy.33 = f32[4,256,8,128]{3,2,1,0:T(8,128)} copy(f32[4,256,8,128]{3,1,2,0:T(8,128)S(1)} %maximum_add_fusion) | data formatting | bytes 8388608 | tf_op jit(solution)/shard_map/add | solution.py:59
  (16 shorter events, 0.1 us)
Async XLA Ops:
  0.0 123.6 %copy-start = (bf16[7,64,2048]{2,1,0:T(8,128)(2,1)S(1)}, bf16[7,64,2048]{2,1,0:T(8,128)(2,1)}, u32[]{:S(2)}) copy-start(bf16[7,64,2048]{2,1,0:T(8,128)(2,1)} %param.15) | copy-start | bytes 5505028
  70.4 4.7 %copy-start.1 = (f32[256,2]{0,1:T(2,128)S(1)}, f32[256,2]{0,1:T(2,128)}, u32[]{:S(2)}) copy-start(f32[256,2]{0,1:T(2,128)} %param.11) | copy-start | bytes 6148
  70.4 36.0 %all-to-all-start.1 = ((bf16[32,24,1536]{2,1,0:T(8,128)(2,1)}), bf16[32,24,1536]{2,1,0:T(8,128)(2,1)}, u32[]{:S(2)}, u32[]{:S(2)}) async-start(bf16[32,24,1536]{2,1,0:T(8,128)(2,1)} %bitcast.90), calls=%async_computation.1 | async-start | bytes 4718592 | tf_op jit(solution)/shard_map/all_to_all | solution.py:95
  112.0 11.6 %copy-start.2 = (f32[2048]{0:T(1024)S(1)}, f32[2048]{0:T(1024)}, u32[]{:S(2)}) copy-start(f32[2048]{0:T(1024)} %param.16) | copy-start | bytes 24580
  115.6 4.6 %collective-permute-start = (bf16[3,64]{0,1:T(8,128)(2,1)S(1)}, bf16[3,64]{0,1:T(8,128)(2,1)S(1)}, u32[]{:S(2)}, u32[]{:S(2)}) collective-permute-start(bf16[3,64]{0,1:T(8,128)(2,1)S(1)} %get-tuple-element.7), channel_id=1, source_target_pairs={{0,1},{1,2},{2,3},{3,4},{4,5},{5,6},{6,7},{7,8},{8,9},{9,10},{10,1... | collective-permute-start | bytes 1160 | tf_op jit(solution)/shard_map/ppermute | solution.py:14
  118.0 5.1 %collective-permute-start.1 = (bf16[3,64]{0,1:T(8,128)(2,1)S(1)}, bf16[3,64]{0,1:T(8,128)(2,1)S(1)}, u32[]{:S(2)}, u32[]{:S(2)}) collective-permute-start(bf16[3,64]{0,1:T(8,128)(2,1)S(1)} %get-tuple-element.8), channel_id=1, source_target_pairs={{1,0},{2,1},{3,2},{4,3},{5,4},{6,5},{7,6},{8,7},{9,8},{10,9},{11,1... | collective-permute-start | bytes 1160 | tf_op jit(solution)/shard_map/ppermute | solution.py:15
  132.4 4.3 %collective-permute-start.2 = (bf16[1,2048]{1,0:T(2,128)(2,1)S(1)}, bf16[1,2048]{1,0:T(2,128)(2,1)S(1)}, u32[]{:S(2)}, u32[]{:S(2)}) collective-permute-start(bf16[1,2048]{1,0:T(2,128)(2,1)S(1)} %get-tuple-element.5), channel_id=1, source_target_pairs={{0,1},{1,2},{2,3},{3,4},{4,5},{5,6},{6,7},{7,8},{8,9},{9,10},{10,1... | collective-permute-start | bytes 12296 | tf_op jit(solution)/shard_map/ppermute | solution.py:14
  134.3 5.0 %collective-permute-start.3 = (bf16[1,2048]{1,0:T(2,128)(2,1)S(1)}, bf16[1,2048]{1,0:T(2,128)(2,1)S(1)}, u32[]{:S(2)}, u32[]{:S(2)}) collective-permute-start(bf16[1,2048]{1,0:T(2,128)(2,1)S(1)} %get-tuple-element.6), channel_id=1, source_target_pairs={{1,0},{2,1},{3,2},{4,3},{5,4},{6,5},{7,6},{8,7},{9,8},{10,9},{11,1... | collective-permute-start | bytes 12296 | tf_op jit(solution)/shard_map/ppermute | solution.py:15
  139.3 54.9 %slice-start = ((s8[8388608]{0:T(1024)(128)(4,1)}), s8[4194304]{0:T(1024)(128)(4,1)S(1)}, s32[]{:S(2)}) async-start(s8[8388608]{0:T(1024)(128)(4,1)} %bitcast.96), calls=%async_computation.3 | async-start | bytes 8388608
  140.1 54.1 %slice-start.1 = ((s8[8388608]{0:T(1024)(128)(4,1)}), s8[4194304]{0:T(1024)(128)(4,1)S(1)}, s32[]{:S(2)}) async-start(s8[8388608]{0:T(1024)(128)(4,1)} %bitcast.96), calls=%async_computation.4 | async-start | bytes 8388608
